TPU v7x, 32 devices: a whole 2x2x4 slice. The times are simulated.
32 devices in a mesh: row: 2 (over y), col: 16 (over z, x, core).
Axes of the slice: x: 2, y: 2, z: 4, core: 2. Of those that a mesh axis runs over, the one named last changes fastest.
Arguments:
- velocity: bfloat16 [3, 512, 1024, 256], P(None, 'row', 'col'), may hold values from -6 to 6
- adj_temp: bfloat16 [512, 1024, 256], P('row', 'col'), may hold values from -6 to 6
- radial_div: bfloat16 [256, 256], replicated, may hold values from -0.375 to 0.375
- reciprocal_distance: float32 [256], replicated, may hold values from 0.002 to 0.02
- radial_basis: bfloat16 [168, 256, 256], P('row'), may hold values from -0.375 to 0.375
- radial_eig: float32 [168, 256], P('row'), may hold values from 0.5 to 8
- axial_diff: bfloat16 [1024, 1024], replicated, may hold values from -0.1875 to 0.1875
- axial_basis: bfloat16 [1024, 1024], replicated, may hold values from -0.1875 to 0.1875
- axial_eig: float32 [1024], replicated, may hold values from 0.5 to 8
Outputs:
- new_temp: float32 [168, 2, 1024, 256], P('row', None, 'col')
All inputs are finite; a program needn't handle non-finite values.
Results may differ from a plain program's by a relative error of at most 0.0055.
Values may be sent and summed in bfloat16 or wider, within the bound.
A program may use at most 256 MiB of HBM per device.

v0:
```python
import functools
import math

import jax
import jax.numpy as jnp
from jax import lax
from jax.experimental import pallas as pl
from jax.experimental.pallas import tpu as pltpu
from jax.sharding import PartitionSpec as P


HEAT_OFFSET = 1.0
BF = jnp.bfloat16
F32 = jnp.float32


def wave_rows(first_mode, mode_count, first_angle, angle_count, circle):
    mode_ids = first_mode + jnp.arange(mode_count, dtype=jnp.int32)
    angle_ids = first_angle + jnp.arange(angle_count, dtype=jnp.int32)
    phase_index = mode_ids[:, None] * angle_ids[None, :] % circle
    angle_value = phase_index.astype(F32) * (2.0 * math.pi / circle)
    norm_factor = 1.0 / math.sqrt(circle)
    table = jnp.stack(
        [jnp.cos(angle_value) * norm_factor, -jnp.sin(angle_value) * norm_factor], axis=1
    )
    return table.astype(BF)


def chunk_count(modes):
    return max(c for c in range(1, 5) if modes % c == 0)


def round_up(value, unit):
    return -(-value // unit) * unit


def sums_kernel(modes, padded, vel_ref, adj_ref, div_ref, table_ref, scale_ref, *refs):
    *out_refs, field_s, sum_s = refs
    angles, block, radial = adj_ref.shape
    adj = adj_ref[...].astype(F32)
    for f in range(3):
        flux = (vel_ref[f].astype(F32) * adj).astype(BF)
        if f == 0:
            moved = lax.dot_general(
                flux.reshape(angles * block, radial),
                div_ref[...],
                (((1,), (1,)), ((), ())),
                preferred_element_type=F32,
            ).reshape(angles, block, radial)
            flux = (HEAT_OFFSET * adj + moved).astype(BF)
        field_s[f] = jnp.swapaxes(flux, 0, 1)

    def one(z, carry):
        heat, turn, flux = (
            jnp.dot(table_ref[...], field_s[f, z], preferred_element_type=F32) for f in range(3)
        )
        scale = scale_ref[...]
        sum_s[0, z] = heat[:padded] - scale * turn[padded:]
        sum_s[1, z] = flux[:padded]
        sum_s[2, z] = heat[padded:] + scale * turn[:padded]
        sum_s[3, z] = flux[padded:]
        return carry

    lax.fori_loop(0, block, one, 0)
    for k in range(4):
        turned = jnp.swapaxes(sum_s[k], 0, 1)
        step = modes // len(out_refs)
        for c, out_ref in enumerate(out_refs):
            out_ref[:, k // 2, k % 2] = turned[c * step : (c + 1) * step].astype(BF)


def azimuth_sums(velocity, adj_temp, radial_div, table, mode_values, reciprocal_distance, parts):
    modes = table.shape[0]
    angles, own_axial, radial = adj_temp.shape
    padded = round_up(modes, 8)
    block = 16 if own_axial % 16 == 0 else own_axial
    table = jnp.pad(jnp.moveaxis(table, 1, 0), ((0, 0), (0, padded - modes), (0, 0)))
    table = table.reshape(2 * padded, angles)
    scale = jnp.pad(
        mode_values[:, None] * reciprocal_distance[None], ((0, padded - modes), (0, 0))
    )
    flops = 2 * own_axial * radial * angles * (radial + 6 * padded)
    return pl.pallas_call(
        functools.partial(sums_kernel, modes, padded),
        grid=(own_axial // block,),
        in_specs=[
            pl.BlockSpec((3, angles, block, radial), lambda z: (0, 0, z, 0)),
            pl.BlockSpec((angles, block, radial), lambda z: (0, z, 0)),
            pl.BlockSpec((radial, radial), lambda z: (0, 0)),
            pl.BlockSpec((2 * padded, angles), lambda z: (0, 0)),
            pl.BlockSpec((padded, radial), lambda z: (0, 0)),
        ],
        out_specs=[
            pl.BlockSpec((modes // parts, 2, 2, block, radial), lambda z: (0, 0, 0, z, 0))
        ]
        * parts,
        out_shape=[jax.ShapeDtypeStruct((modes // parts, 2, 2, own_axial, radial), BF)] * parts,
        scratch_shapes=[
            pltpu.VMEM((3, block, angles, radial), BF),
            pltpu.VMEM((4, block, padded, radial), F32),
        ],
        compiler_params=pltpu.CompilerParams(vmem_limit_bytes=60 * 2**20),
        cost_estimate=pl.CostEstimate(
            flops=flops, bytes_accessed=8 * angles * own_axial * radial, transcendentals=0
        ),
        name="sums",
    )(velocity, adj_temp, radial_div, table, scale)


def radial_kernel(count, *refs):
    own_ref, others, basis_ref, out_ref = refs[0], refs[1:-2], refs[-2], refs[-1]
    radial = basis_ref.shape[1]
    for m in range(count):
        total = own_ref[m].astype(F32)
        for other in others:
            total = total + other[m].astype(F32)
        width = total.shape[0] * total.shape[1] * total.shape[2]
        hat = lax.dot_general(
            basis_ref[m],
            total.astype(BF).reshape(width, radial),
            (((0,), (1,)), ((), ())),
            preferred_element_type=F32,
        ).astype(BF)
        out_ref[:, m] = hat.reshape(out_ref.shape[0], out_ref.shape[2], width)


def radial_forward(own, others, basis, first, step, col_total):
    radial = basis.shape[1]
    width = 4 * own.shape[3]
    count = max(c for c in range(1, 8) if step % c == 0)
    skip = first // count
    field = (count, 2, 2, own.shape[3], radial)
    return pl.pallas_call(
        functools.partial(radial_kernel, count),
        grid=(step // count,),
        in_specs=[pl.BlockSpec(field, lambda m: (m, 0, 0, 0, 0)) for _ in (own, *others)]
        + [pl.BlockSpec((count, radial, radial), lambda m: (m + skip, 0, 0))],
        out_specs=pl.BlockSpec(
            (col_total, count, radial // col_total, width), lambda m: (0, m, 0, 0)
        ),
        out_shape=jax.ShapeDtypeStruct((col_total, step, radial // col_total, width), BF),
        compiler_params=pltpu.CompilerParams(vmem_limit_bytes=60 * 2**20),
        cost_estimate=pl.CostEstimate(
            flops=2 * step * radial * radial * width,
            bytes_accessed=2 * step * radial * (radial + 3 * width),
            transcendentals=0,
        ),
        name="radial",
    )(own, *others, basis)


def axial_kernel(lines_ref, forward_ref, basis_ref, radial_ref, axial_ref, out_ref):
    col_total, count, own_count, width = lines_ref.shape
    half = width // 2
    quarter = width // 4
    rows = count * own_count
    lines = jnp.concatenate(
        [
            jnp.concatenate(
                [
                    lines_ref[s, :, :, p * half : (p + 1) * half].reshape(rows, half)
                    for s in range(col_total)
                ],
                axis=1,
            )
            for p in range(2)
        ],
        axis=0,
    )
    coefficients = jnp.dot(lines, forward_ref[...], preferred_element_type=F32)
    eigen = radial_ref[...] + axial_ref[...] + HEAT_OFFSET
    coefficients = jnp.concatenate([coefficients[:rows] / eigen, coefficients[rows:] / eigen], axis=0)
    returned = lax.dot_general(
        coefficients.astype(BF),
        basis_ref[...],
        (((1,), (1,)), ((), ())),
        preferred_element_type=F32,
    )
    for s in range(col_total):
        own = slice(s * quarter, (s + 1) * quarter)
        pair = jnp.concatenate([returned[:rows, own], returned[rows:, own]], axis=1)
        out_ref[s] = pair.astype(BF).reshape(count, own_count, half)


def axial_solve(lines, forward, axial_basis, radial_values, axial_eig):
    col_total, step, own_count, width = lines.shape
    points = axial_basis.shape[0]
    count = max(c for c in range(1, 8) if step % c == 0)
    rows = step * own_count
    return pl.pallas_call(
        axial_kernel,
        grid=(step // count,),
        in_specs=[
            pl.BlockSpec((col_total, count, own_count, width), lambda m: (0, m, 0, 0)),
            pl.BlockSpec((2 * points, points), lambda m: (0, 0)),
            pl.BlockSpec((points, points), lambda m: (0, 0)),
            pl.BlockSpec((count * own_count, 1), lambda m: (m, 0)),
            pl.BlockSpec((1, points), lambda m: (0, 0)),
        ],
        out_specs=pl.BlockSpec((col_total, count, own_count, width // 2), lambda m: (0, m, 0, 0)),
        out_shape=jax.ShapeDtypeStruct((col_total, step, own_count, width // 2), BF),
        compiler_params=pltpu.CompilerParams(vmem_limit_bytes=60 * 2**20),
        cost_estimate=pl.CostEstimate(
            flops=12 * rows * points * points,
            bytes_accessed=6 * points * points + 6 * rows * points,
            transcendentals=0,
        ),
        name="axial",
    )(lines, forward, axial_basis, radial_values.reshape(rows, 1), axial_eig.reshape(1, points))


def last_kernel(count, returned_ref, basis_ref, *refs):
    out_ref = refs[-1]
    for m in range(count):
        lines = returned_ref[:, m]
        lines = lines.reshape(lines.shape[0] * lines.shape[1], lines.shape[2])
        out_ref[m] = lax.dot_general(
            lines, basis_ref[m], (((0,), (1,)), ((), ())), preferred_element_type=F32
        ).reshape(out_ref.shape[1:])


def radial_back(returned, basis, before, first):
    col_total, step, own_count, width = returned.shape
    modes, radial, _ = basis.shape
    count = max(c for c in range(1, 8) if step % c == 0)
    skip = first // count
    return pl.pallas_call(
        functools.partial(last_kernel, count),
        grid=(step // count,),
        in_specs=[
            pl.BlockSpec((col_total, count, own_count, width), lambda m: (0, m, 0, 0)),
            pl.BlockSpec((count, radial, radial), lambda m: (m + skip, 0, 0)),
        ]
        + [pl.BlockSpec(memory_space=pl.ANY) for _ in before],
        out_specs=pl.BlockSpec((count, 2, width // 2, radial), lambda m: (m + skip, 0, 0, 0)),
        out_shape=jax.ShapeDtypeStruct((modes, 2, width // 2, radial), F32),
        input_output_aliases={2: 0} if before else {},
        compiler_params=pltpu.CompilerParams(vmem_limit_bytes=60 * 2**20),
        cost_estimate=pl.CostEstimate(
            flops=2 * step * radial * radial * width,
            bytes_accessed=2 * step * radial * (radial + 3 * width),
            transcendentals=0,
        ),
        name="last",
    )(returned, basis, *before)


def body(
    velocity,
    adj_temp,
    radial_div,
    reciprocal_distance,
    radial_basis,
    radial_eig,
    axial_diff,
    axial_basis,
    axial_eig,
):
    row_total = lax.axis_size("row")
    col_total = lax.axis_size("col")
    row_place = lax.axis_index("row")
    col_place = lax.axis_index("col")
    modes = radial_basis.shape[0]
    angles, own_axial, radial_points = adj_temp.shape
    axial_points = axial_basis.shape[0]
    own_count = radial_points // col_total
    circle = angles * row_total
    parts = chunk_count(modes)
    step = modes // parts

    def partial_sums(place):
        table = wave_rows(place * modes, modes, row_place * angles, angles, circle)
        mode_values = (place * modes + jnp.arange(modes, dtype=jnp.int32)).astype(F32)
        return azimuth_sums(
            velocity, adj_temp, radial_div, table, mode_values, reciprocal_distance, parts
        )

    arrived = [[] for _ in range(parts)]
    for shift in range(1, row_total):
        sums = partial_sums((row_place + shift) % row_total)
        pairs = [(a, (a + shift) % row_total) for a in range(row_total)]
        for c in range(parts):
            arrived[c].append(lax.ppermute(sums[c], "row", pairs))
    own = partial_sums(row_place)

    returning = jnp.einsum("zj,zk->jk", axial_diff, axial_basis, preferred_element_type=F32)
    forward = jnp.stack(
        [
            axial_basis.reshape(col_total, own_axial, axial_points),
            returning.astype(BF).reshape(col_total, own_axial, axial_points),
        ],
        axis=1,
    )
    axial_blocks = axial_basis.reshape(col_total, own_axial, axial_points)
    radial_values = lax.dynamic_slice_in_dim(radial_eig, col_place * own_count, own_count, 1)

    fits = own_axial % 64 == 0 and own_count % 16 == 0
    outs = []
    new_temp = ()
    for c in range(parts):
        part = slice(c * step, (c + 1) * step)
        hat = radial_forward(own[c], arrived[c], radial_basis, c * step, step, col_total)
        lines = lax.all_to_all(hat, "col", split_axis=0, concat_axis=0, tiled=True)
        if fits:
            returned = axial_solve(
                lines,
                forward.reshape(2 * axial_points, axial_points),
                axial_basis,
                radial_values[part],
                axial_eig,
            )
        else:
            lines = lines.reshape(col_total, step, own_count, 2, 2, own_axial)
            coefficients = jnp.einsum(
                "smxpfy,sfyk->pmxk", lines, forward, preferred_element_type=F32
            )
            coefficients = coefficients / (
                radial_values[part][None, :, :, None] + axial_eig + HEAT_OFFSET
            )
            returned = jnp.einsum(
                "pmxk,syk->smxpy", coefficients.astype(BF), axial_blocks, preferred_element_type=F32
            ).astype(BF)
            returned = returned.reshape(col_total, step, own_count, 2 * own_axial)
        returned = lax.all_to_all(returned, "col", split_axis=0, concat_axis=0, tiled=True)
        if fits:
            new_temp = (radial_back(returned, radial_basis, new_temp, c * step),)
            continue
        returned = jnp.moveaxis(returned, 0, 1).reshape(step, radial_points, 2 * own_axial)
        outs.append(
            jnp.einsum("miw,mri->mwr", returned, radial_basis[part], preferred_element_type=F32).reshape(
                step, 2, own_axial, radial_points
            )
        )
    return new_temp[0] if fits else jnp.concatenate(outs, axis=0)


def both_sums_kernel(modes, padded, vel_ref, adj_ref, div_ref, table_ref, scale_ref, *refs):
    *out_refs, field_s, sum_s = refs
    angles, block, radial = adj_ref.shape
    adj = adj_ref[...].astype(F32)
    for f in range(3):
        flux = (vel_ref[f].astype(F32) * adj).astype(BF)
        if f == 0:
            moved = lax.dot_general(
                flux.reshape(angles * block, radial),
                div_ref[...],
                (((1,), (1,)), ((), ())),
                preferred_element_type=F32,
            ).reshape(angles, block, radial)
            flux = (HEAT_OFFSET * adj + moved).astype(BF)
        field_s[f] = jnp.swapaxes(flux, 0, 1)

    def one(z, carry):
        heat, turn, flux = (
            jnp.dot(table_ref[...], field_s[f, z], preferred_element_type=F32) for f in range(3)
        )
        for d in range(len(out_refs)):
            re = slice(2 * d * padded, (2 * d + 1) * padded)
            im = slice((2 * d + 1) * padded, (2 * d + 2) * padded)
            scale = scale_ref[d]
            sum_s[4 * d, z] = heat[re] - scale * turn[im]
            sum_s[4 * d + 1, z] = flux[re]
            sum_s[4 * d + 2, z] = heat[im] + scale * turn[re]
            sum_s[4 * d + 3, z] = flux[im]
        return carry

    lax.fori_loop(0, block, one, 0)
    for d, out_ref in enumerate(out_refs):
        for k in range(4):
            turned = jnp.swapaxes(sum_s[4 * d + k], 0, 1)
            out_ref[:, k // 2, k % 2] = turned[:modes].astype(BF)


def both_sums(velocity, adj_temp, radial_div, tables, mode_values, reciprocal_distance):
    dests, modes = mode_values.shape
    angles, own_axial, radial = adj_temp.shape
    padded = round_up(modes, 8)
    block = 16 if own_axial % 16 == 0 else own_axial
    table = jnp.pad(jnp.moveaxis(tables, 2, 1), ((0, 0), (0, 0), (0, padded - modes), (0, 0)))
    table = table.reshape(dests * 2 * padded, angles)
    scale = mode_values[:, :, None] * reciprocal_distance[None, None]
    scale = jnp.pad(scale, ((0, 0), (0, padded - modes), (0, 0)))
    flops = 2 * own_axial * radial * angles * (radial + 6 * padded * dests)
    return pl.pallas_call(
        functools.partial(both_sums_kernel, modes, padded),
        grid=(own_axial // block,),
        in_specs=[
            pl.BlockSpec((3, angles, block, radial), lambda z: (0, 0, z, 0)),
            pl.BlockSpec((angles, block, radial), lambda z: (0, z, 0)),
            pl.BlockSpec((radial, radial), lambda z: (0, 0)),
            pl.BlockSpec((dests * 2 * padded, angles), lambda z: (0, 0)),
            pl.BlockSpec((dests, padded, radial), lambda z: (0, 0, 0)),
        ],
        out_specs=[pl.BlockSpec((modes, 2, 2, block, radial), lambda z: (0, 0, 0, z, 0))] * dests,
        out_shape=[jax.ShapeDtypeStruct((modes, 2, 2, own_axial, radial), BF)] * dests,
        scratch_shapes=[
            pltpu.VMEM((3, block, angles, radial), BF),
            pltpu.VMEM((4 * dests, block, padded, radial), F32),
        ],
        compiler_params=pltpu.CompilerParams(vmem_limit_bytes=60 * 2**20),
        cost_estimate=pl.CostEstimate(
            flops=flops, bytes_accessed=8 * angles * own_axial * radial, transcendentals=0
        ),
        name="sums",
    )(velocity, adj_temp, radial_div, table, scale)


MESH = pl.DeviceIdType.MESH


def solve_kernel(
    chunks,
    lags,
    own_hbm,
    other_hbm,
    basis_hbm,
    forward_ref,
    back_ref,
    radial_ref,
    axial_ref,
    out_hbm,
    field_s,
    lines_s,
    cross_s,
    back_s,
    part_s,
    cross_o,
    back_o,
    own_s,
    basis_s,
    again_s,
    out_s,
    row_send,
    row_recv,
    ahead_send,
    ahead_recv,
    cross_send,
    cross_recv,
    back_send,
    back_recv,
    load_sem,
    out_sem,
):
    group, modes, block, width = lines_s.shape
    count = modes // chunks
    half = width // 2
    quarter = width // 4
    rows = count * block
    lag_axial, lag_add, lag_last = lags
    row_place = lax.axis_index("row")
    col_place = lax.axis_index("col")
    side = col_place // group
    place = col_place % group
    across = {"row": 1 - row_place}
    mirror = {"col": (1 - side) * group + place}

    def peer(k):
        return (place + k) % group

    def peer_id(k):
        return {"col": side * group + peer(k)}

    def span(c):
        return pl.ds(c * count, count)

    def row_copy(c):
        return pltpu.make_async_remote_copy(
            src_ref=other_hbm.at[span(c)],
            dst_ref=field_s.at[span(c)],
            send_sem=row_send.at[c],
            recv_sem=row_recv.at[c],
            device_id=across,
            device_id_type=MESH,
        )

    def ahead_copy(c, k):
        first = pl.multiple_of(peer(k) * block, block)
        return pltpu.make_async_remote_copy(
            src_ref=field_s.at[span(c), pl.ds(first, block)],
            dst_ref=lines_s.at[place, span(c)],
            send_sem=ahead_send.at[c % 2, k],
            recv_sem=ahead_recv.at[c, k],
            device_id=peer_id(k),
            device_id_type=MESH,
        )

    def cross_copy(c):
        return pltpu.make_async_remote_copy(
            src_ref=cross_o.at[c % 2],
            dst_ref=cross_s.at[c],
            send_sem=cross_send.at[c % 2],
            recv_sem=cross_recv.at[c],
            device_id=mirror,
            device_id_type=MESH,
        )

    def back_copy(c, k):
        return pltpu.make_async_remote_copy(
            src_ref=back_o.at[c % 2, peer(k)],
            dst_ref=back_s.at[place, span(c)],
            send_sem=back_send.at[c % 2, k],
            recv_sem=back_recv.at[c, k],
            device_id=peer_id(k),
            device_id_type=MESH,
        )

    def own_load(c):
        return pltpu.make_async_copy(own_hbm.at[span(c)], own_s.at[c % 2], load_sem.at[0, c % 2])

    def basis_load(c):
        return pltpu.make_async_copy(basis_hbm.at[span(c)], basis_s.at[c % 2], load_sem.at[1, c % 2])

    def again_load(c):
        return pltpu.make_async_copy(basis_hbm.at[span(c)], again_s.at[c % 2], load_sem.at[2, c % 2])

    def out_copy(c):
        return pltpu.make_async_copy(out_s.at[c % 2], out_hbm.at[span(c)], out_sem.at[c % 2])

    others = range(1, group)
    own_load(0).start()
    basis_load(0).start()
    again_load(0).start()
    barrier = pltpu.get_barrier_semaphore()
    for device in [across, mirror] + [peer_id(k) for k in others]:
        pl.semaphore_signal(barrier, inc=1, device_id=device, device_id_type=MESH)
    pl.semaphore_wait(barrier, group + 1)

    def send_row(c, carry):
        row_copy(c).start()
        return carry

    lax.fori_loop(0, chunks, send_row, 0)

    def radial_part(c):
        own_load(c).wait()
        basis_load(c).wait()

        @pl.when(c + 1 < chunks)
        def _():
            own_load(c + 1).start()
            basis_load(c + 1).start()

        @pl.when(c >= 2)
        def _():
            for k in others:
                ahead_copy(c - 2, k).wait_send()

        row_copy(c).wait_recv()
        for m in range(count):
            mode = c * count + m
            total = own_s[c % 2, m].astype(F32) + field_s[mode].astype(F32)
            hat = lax.dot_general(
                basis_s[c % 2, m],
                total.astype(BF),
                (((0,), (1,)), ((), ())),
                preferred_element_type=F32,
            )
            field_s[mode] = hat.astype(BF)
        mine = pl.multiple_of(place * block, block)
        lines_s[place, span(c)] = field_s[span(c), pl.ds(mine, block), :]
        for k in others:
            ahead_copy(c, k).start()

    def axial_part(c):
        for k in others:
            ahead_copy(c, k).wait_recv()

        @pl.when(c >= 2)
        def _():
            cross_copy(c - 2).wait_send()

        first = pl.multiple_of(c * rows, rows)
        eigen = radial_ref[pl.ds(first, rows), :] + axial_ref[...] + HEAT_OFFSET
        returned = []
        for p in range(2):
            lines = jnp.concatenate(
                [
                    lines_s[s, span(c), :, p * half : (p + 1) * half].reshape(rows, half)
                    for s in range(group)
                ],
                axis=1,
            )
            coefficients = jnp.dot(lines, forward_ref[...], preferred_element_type=F32) / eigen
            returned.append(
                lax.dot_general(
                    coefficients.astype(BF),
                    back_ref[...],
                    (((1,), (1,)), ((), ())),
                    preferred_element_type=F32,
                )
            )
        for s in range(2 * group):
            own = slice(s * quarter, (s + 1) * quarter)
            pair = jnp.concatenate([returned[0][:, own], returned[1][:, own]], axis=1)
            pair = pair.reshape(count, block, half)
            if s < group:
                part_s[c % part_s.shape[0], s] = pair
            else:
                cross_o[c % 2, s - group] = pair.astype(BF)
        cross_copy(c).start()

    def add_part(c):
        cross_copy(c).wait_recv()

        @pl.when(c >= 2)
        def _():
            for k in others:
                back_copy(c - 2, k).wait_send()

        total = part_s[c % part_s.shape[0]] + cross_s[c].astype(F32)
        back_o[c % 2] = total.astype(BF)
        back_s[place, span(c)] = back_o[c % 2, place]
        for k in others:
            back_copy(c, k).start()

    def last_part(c):
        again_load(c).wait()

        @pl.when(c + 1 < chunks)
        def _():
            again_load(c + 1).start()

        @pl.when(c >= 2)
        def _():
            out_copy(c - 2).wait()

        for k in others:
            back_copy(c, k).wait_recv()
        for m in range(count):
            lines = back_s[:, c * count + m].reshape(group * block, half)
            out_s[c % 2, m] = lax.dot_general(
                lines, again_s[c % 2, m], (((0,), (1,)), ((), ())), preferred_element_type=F32
            ).reshape(out_s.shape[2:])
        out_copy(c).start()

    def step(s, carry):
        for part, lag in (
            (radial_part, 0),
            (add_part, lag_add),
            (axial_part, lag_axial),
            (last_part, lag_last),
        ):
            pl.when((s >= lag) & (s < chunks + lag))(functools.partial(part, s - lag))
        return carry

    lax.fori_loop(0, chunks + lag_last, step, 0)

    def row_done(c, carry):
        row_copy(c).wait_send()
        return carry

    lax.fori_loop(0, chunks, row_done, 0)
    for c in range(chunks - 2, chunks):
        for k in others:
            ahead_copy(c, k).wait_send()
            back_copy(c, k).wait_send()
        cross_copy(c).wait_send()
        out_copy(c).wait()


def solve(own, other, basis, forward, back, radial_values, axial_eig, group, chunks, lags):
    modes, radial, _ = basis.shape
    width = own.shape[1]
    points = forward.shape[1]
    block = radial // group
    count = modes // chunks
    half = width // 2
    anywhere = pl.BlockSpec(memory_space=pl.ANY)
    vmem = pl.BlockSpec(memory_space=pltpu.VMEM)
    own_axial = width // 4
    dma = pltpu.SemaphoreType.DMA
    lines = 2 * modes * block
    sent = 2 * modes * radial * width * 3
    return pl.pallas_call(
        functools.partial(solve_kernel, chunks, lags),
        in_specs=[anywhere] * 3 + [vmem] * 4,
        out_specs=anywhere,
        out_shape=jax.ShapeDtypeStruct((modes, 2, own_axial, radial), F32),
        scratch_shapes=[
            pltpu.VMEM((modes, width, radial), BF),
            pltpu.VMEM((group, modes, block, width), BF),
            pltpu.VMEM((chunks, group, count, block, half), BF),
            pltpu.VMEM((group, modes, block, half), BF),
            pltpu.VMEM((lags[1] - lags[0], group, count, block, half), F32),
            pltpu.VMEM((2, group, count, block, half), BF),
            pltpu.VMEM((2, group, count, block, half), BF),
            pltpu.VMEM((2, count, width, radial), BF),
            pltpu.VMEM((2, count, radial, radial), BF),
            pltpu.VMEM((2, count, radial, radial), BF),
            pltpu.VMEM((2, count, 2, own_axial, radial), F32),
            dma((chunks,)),
            dma((chunks,)),
            dma((2, group)),
            dma((chunks, group)),
            dma((2,)),
            dma((chunks,)),
            dma((2, group)),
            dma((chunks, group)),
            dma((3, 2)),
            dma((2,)),
        ],
        compiler_params=pltpu.CompilerParams(
            collective_id=0, has_side_effects=True, vmem_limit_bytes=63 * 2**20
        ),
        cost_estimate=pl.CostEstimate(
            flops=4 * lines * points * points + 6 * modes * radial * radial * width,
            bytes_accessed=sent,
            transcendentals=0,
        ),
        name="solve",
    )(own, other, basis, forward, back, radial_values.reshape(modes * block, 1), axial_eig[None])


CHUNK_MODES = 7
LAGS = (1, 2, 3)


def fused_body(
    velocity,
    adj_temp,
    radial_div,
    reciprocal_distance,
    radial_basis,
    radial_eig,
    axial_diff,
    axial_basis,
    axial_eig,
):
    row_total = lax.axis_size("row")
    group = lax.axis_size("col") // 2
    row_place = lax.axis_index("row")
    col_place = lax.axis_index("col")
    side, place = col_place // group, col_place % group
    modes = radial_basis.shape[0]
    angles, own_axial, radial_points = adj_temp.shape
    axial_points = axial_basis.shape[0]
    circle = angles * row_total
    block = radial_points // group
    dests = (row_place, 1 - row_place)
    tables = jnp.stack(
        [wave_rows(d * modes, modes, row_place * angles, angles, circle) for d in dests]
    )
    mode_values = jnp.stack(
        [(d * modes + jnp.arange(modes, dtype=jnp.int32)).astype(F32) for d in dests]
    )
    own, other = both_sums(
        velocity, adj_temp, radial_div, tables, mode_values, reciprocal_distance
    )
    own = own.reshape(modes, 4 * own_axial, radial_points)
    other = other.reshape(modes, 4 * own_axial, radial_points)

    half_points = axial_points // 2
    near = lax.dynamic_slice_in_dim(axial_basis, side * half_points, half_points, 0)
    far = lax.dynamic_slice_in_dim(axial_basis, (1 - side) * half_points, half_points, 0)
    near_diff = lax.dynamic_slice_in_dim(axial_diff, side * half_points, half_points, 1)
    turned = jnp.einsum("zj,zk->jk", near_diff, axial_basis, preferred_element_type=F32).astype(BF)
    forward = jnp.stack(
        [x.reshape(group, own_axial, axial_points) for x in (near, turned)], axis=1
    ).reshape(axial_points, axial_points)
    back = jnp.concatenate([near, far], axis=0)
    radial_values = lax.dynamic_slice_in_dim(radial_eig, place * block, block, 1)
    chunks = modes // CHUNK_MODES
    return solve(
        own, other, radial_basis, forward, back, radial_values, axial_eig, group, chunks, LAGS
    )


def solution(mesh):
    in_specs = (
        P(None, "row", "col", None),
        P("row", "col", None),
        P(),
        P(),
        P("row", None, None),
        P("row", None),
        P(),
        P(),
        P(),
    )
    out_specs = P("row", None, "col", None)
    if mesh.shape["row"] == 2 and mesh.shape["col"] == 16:
        return jax.shard_map(
            fused_body, mesh=mesh, in_specs=in_specs, out_specs=out_specs, check_vma=False
        )
    return jax.shard_map(body, mesh=mesh, in_specs=in_specs, out_specs=out_specs, check_vma=False)
```

profile of v0, /device:TPU:0, one launch (start us, length us, event | category | flops | bytes accessed | tf_op | source)
XLA Modules:
  0.0 416.9 jit_solution(9869699571067050845)
XLA Ops:
  0.0 0.0 copy-start
  0.0 0.8 copy-done
  0.9 0.1 constant_dynamic-slice_fusion
  1.0 0.8 fusion.7
  1.8 0.7 pad.8
  2.5 0.8 broadcast_multiply_fusion
  3.3 0.7 pad.9.scale_ref
  4.0 0.0 copy-start.2
  4.0 3.3 convolution_convert_fusion
  7.3 2.5 reshape.398.radial_ref
  9.8 0.0 copy-done.2
  9.8 0.2 constant_dynamic-slice_fusion.1
  10.0 1.5 pad_maximum_fusion
  11.5 1.6 pad_maximum_fusion.1.back_ref
  13.1 46.3 %sums.1 = (bf16[84,2,2,64,256]{4,3,2,1,0:T(8,128)(2,1)}, bf16[84,2,2,64,256]{4,3,2,1,0:T(8,128)(2,1)}) custom-call(bf16[3,256,64,256]{3,2,1,0:T(8,128)(2,1)} %vel_ref.1, bf16[256,64,256]{2,1,0:T(8,128)(2,1)} %adj_ref.1, bf16[256,256]{1,0:T(8,128)(2,1)} %div_ref.1, bf16[352,256]{1,0:T(8,128)(2,1)} %bitcast.23, f32[2,88,256]{2,1,0:T(8,128)} %pad.9.scale_ref), custom_call_target="tpu_custom_call" | custom-call | flops 11005853696 | bytes 33554432 | tf_op jit(solution)/shard_map/sums/pallas_call | solution.py:384
  59.3 347.3 %solve.1 = f32[84,2,64,256]{3,2,1,0:T(8,128)} custom-call(bf16[84,256,256]{2,1,0:T(8,128)(2,1)} %bitcast.25, bf16[84,256,256]{2,1,0:T(8,128)(2,1)} %bitcast.26, bf16[84,256,256]{2,1,0:T(8,128)(2,1)} %basis_hbm.1, bf16[1024,1024]{1,0:T(8,128)(2,1)} %bitcast.22, bf16[1024,1024]{1,0:T(8,128)(2,1)} %pad_maximum_fusion.1.back_ref, ...), custom_call_target="tpu_custom_call" | custom-call | flops 31004295168 | bytes 33030144 | tf_op jit(solution)/shard_map/solve/pallas_call | solution.py:674
  406.7 0.0 copy-start.1
  406.7 10.2 %copy.14 = f32[84,2,64,256]{3,2,1,0:T(8,128)} copy(f32[84,2,64,256]{3,2,1,0:T(8,128)} %solve.1) | data formatting | bytes 22020096
  416.9 0.0 copy-done.1
  (5 shorter events, 0.1 us)
Async XLA Ops:
  0.0 0.9 copy-start
  4.0 5.8 %copy-start.2 = (bf16[1024,1024]{1,0:T(8,128)(2,1)S(1)}, bf16[1024,1024]{1,0:T(8,128)(2,1)}, u32[]{:S(2)}) copy-start(bf16[1024,1024]{1,0:T(8,128)(2,1)} %param.16) | copy-start | bytes 6291460
  406.7 10.2 %copy-start.1 = (f32[84,256]{1,0:T(8,128)S(1)}, f32[84,256]{1,0:T(8,128)}, u32[]{:S(2)}) copy-start(f32[84,256]{1,0:T(8,128)} %param.14) | copy-start | bytes 258052
where the time goes:
time: 418 us; the launch traced here: 417 us
  Pallas kernels  394 us (94%)
  local copies, waits for them, and re-layouts  15.2 us (4%)
  other arithmetic  4.72 us (1%)
    pallas_call x1, Pallas kernels, solve(): pl.pallas_call(functools.partial(solve_kernel, chunks, lags), in_specs=[a...  347 us
    pallas_call x1, Pallas kernels, both_sums(): pl.pallas_call(functools.partial(both_sums_kernel, modes, padded), grid=(...  46.3 us
    unnamed x7, local copies, waits for them, and re-layouts  11.1 us

commit v1 on v0

--- a/solution.py
+++ b/solution.py
@@ -371,15 +371,14 @@
             out_ref[:, k // 2, k % 2] = turned[:modes].astype(BF)
 
 
-def both_sums(velocity, adj_temp, radial_div, tables, mode_values, reciprocal_distance):
-    dests, modes = mode_values.shape
+def both_sums(
+    velocity, adj_temp, radial_div, tables, mode_values, reciprocal_distance, modes
+):
+    dests, padded = mode_values.shape
     angles, own_axial, radial = adj_temp.shape
-    padded = round_up(modes, 8)
     block = 16 if own_axial % 16 == 0 else own_axial
-    table = jnp.pad(jnp.moveaxis(tables, 2, 1), ((0, 0), (0, 0), (0, padded - modes), (0, 0)))
-    table = table.reshape(dests * 2 * padded, angles)
+    table = jnp.moveaxis(tables, 2, 1).reshape(dests * 2 * padded, angles)
     scale = mode_values[:, :, None] * reciprocal_distance[None, None]
-    scale = jnp.pad(scale, ((0, 0), (0, padded - modes), (0, 0)))
     flops = 2 * own_axial * radial * angles * (radial + 6 * padded * dests)
     return pl.pallas_call(
         functools.partial(both_sums_kernel, modes, padded),
@@ -414,10 +413,10 @@
     own_hbm,
     other_hbm,
     basis_hbm,
-    forward_ref,
-    back_ref,
+    diff_hbm,
+    axial_ref,
     radial_ref,
-    axial_ref,
+    eig_ref,
     out_hbm,
     field_s,
     lines_s,
@@ -430,6 +429,8 @@
     basis_s,
     again_s,
     out_s,
+    forward_s,
+    diff_s,
     row_send,
     row_recv,
     ahead_send,
@@ -441,27 +442,50 @@
     load_sem,
     out_sem,
 ):
-    group, modes, block, width = lines_s.shape
+    group, modes, big, width = lines_s.shape
+    radial = field_s.shape[2]
+    team = group // 2
+    small = radial // team - big
+    sizes = (big, small)
+    starts = (0, team * big)
     count = modes // chunks
     half = width // 2
-    quarter = width // 4
-    rows = count * block
+    own_axial = width // 4
+    points = axial_ref.shape[0] // 2
     lag_axial, lag_add, lag_last = lags
     row_place = lax.axis_index("row")
     col_place = lax.axis_index("col")
     side = col_place // group
     place = col_place % group
+    seat = place % team
+    mine = (place // team + 1 - side) % 2
     across = {"row": 1 - row_place}
-    mirror = {"col": (1 - side) * group + place}
-
-    def peer(k):
-        return (place + k) % group
-
-    def peer_id(k):
-        return {"col": side * group + peer(k)}
+
+    def device(which, kind, number):
+        return {"col": which * group + ((kind + 1 + which) % 2) * team + number}
+
+    mirror = device(1 - side, mine, seat)
+
+    def peer_seat(k):
+        return (seat + k) % team
+
+    def place_of(kind, k):
+        return ((kind + 1 + side) % 2) * team + peer_seat(k)
+
+    def each_peer(act):
+        for kind in range(2):
+            for k in range(team):
+                if k == 0:
+                    pl.when(mine != kind)(functools.partial(act, kind, k))
+                else:
+                    act(kind, k)
 
     def span(c):
         return pl.ds(c * count, count)
+
+    def rows_of(kind, number):
+        first = starts[kind] + number * sizes[kind]
+        return pl.ds(pl.multiple_of(first, math.gcd(*sizes)), sizes[kind])
 
     def row_copy(c):
         return pltpu.make_async_remote_copy(
@@ -473,34 +497,55 @@
             device_id_type=MESH,
         )
 
-    def ahead_copy(c, k):
-        first = pl.multiple_of(peer(k) * block, block)
+    def ahead_copy(c, kind, k):
         return pltpu.make_async_remote_copy(
-            src_ref=field_s.at[span(c), pl.ds(first, block)],
-            dst_ref=lines_s.at[place, span(c)],
-            send_sem=ahead_send.at[c % 2, k],
-            recv_sem=ahead_recv.at[c, k],
-            device_id=peer_id(k),
+            src_ref=field_s.at[span(c), rows_of(kind, peer_seat(k))],
+            dst_ref=lines_s.at[place, span(c), pl.ds(0, sizes[kind])],
+            send_sem=ahead_send.at[c % 2, kind, k],
+            recv_sem=ahead_recv.at[c, mine, k],
+            device_id=device(side, kind, peer_seat(k)),
             device_id_type=MESH,
         )
 
-    def cross_copy(c):
+    def ahead_come(c, own_kind, kind, k):
+        part = pl.ds(0, sizes[own_kind])
         return pltpu.make_async_remote_copy(
-            src_ref=cross_o.at[c % 2],
-            dst_ref=cross_s.at[c],
+            src_ref=field_s.at[span(c), part],
+            dst_ref=lines_s.at[place, span(c), part],
+            send_sem=ahead_send.at[c % 2, kind, k],
+            recv_sem=ahead_recv.at[c, kind, k],
+            device_id=device(side, kind, peer_seat(k)),
+            device_id_type=MESH,
+        )
+
+    def cross_copy(c, own_kind):
+        part = pl.ds(0, sizes[own_kind])
+        return pltpu.make_async_remote_copy(
+            src_ref=cross_o.at[c % 2, :, :, part],
+            dst_ref=cross_s.at[c, :, :, part],
             send_sem=cross_send.at[c % 2],
             recv_sem=cross_recv.at[c],
             device_id=mirror,
             device_id_type=MESH,
         )
 
-    def back_copy(c, k):
+    def back_copy(c, own_kind, kind, k):
         return pltpu.make_async_remote_copy(
-            src_ref=back_o.at[c % 2, peer(k)],
-            dst_ref=back_s.at[place, span(c)],
-            send_sem=back_send.at[c % 2, k],
-            recv_sem=back_recv.at[c, k],
-            device_id=peer_id(k),
+            src_ref=back_o.at[c % 2, place_of(kind, k), :, pl.ds(0, sizes[own_kind])],
+            dst_ref=back_s.at[span(c), rows_of(own_kind, seat)],
+            send_sem=back_send.at[c % 2, kind, k],
+            recv_sem=back_recv.at[c, own_kind, k],
+            device_id=device(side, kind, peer_seat(k)),
+            device_id_type=MESH,
+        )
+
+    def back_come(c, kind, k):
+        return pltpu.make_async_remote_copy(
+            src_ref=back_o.at[c % 2, place, :, pl.ds(0, sizes[kind])],
+            dst_ref=back_s.at[span(c), rows_of(kind, seat)],
+            send_sem=back_send.at[c % 2, kind, k],
+            recv_sem=back_recv.at[c, kind, k],
+            device_id=device(side, kind, peer_seat(k)),
             device_id_type=MESH,
         )
 
@@ -516,13 +561,20 @@
     def out_copy(c):
         return pltpu.make_async_copy(out_s.at[c % 2], out_hbm.at[span(c)], out_sem.at[c % 2])
 
-    others = range(1, group)
+    near = pl.multiple_of(side * points, points)
+    diff_load = pltpu.make_async_copy(diff_hbm.at[:, pl.ds(near, points)], diff_s, load_sem.at[3, 0])
+    diff_load.start()
     own_load(0).start()
     basis_load(0).start()
     again_load(0).start()
     barrier = pltpu.get_barrier_semaphore()
-    for device in [across, mirror] + [peer_id(k) for k in others]:
-        pl.semaphore_signal(barrier, inc=1, device_id=device, device_id_type=MESH)
+
+    def greet(target):
+        pl.semaphore_signal(barrier, inc=1, device_id=target, device_id_type=MESH)
+
+    greet(across)
+    greet(mirror)
+    each_peer(lambda kind, k: greet(device(side, kind, peer_seat(k))))
     pl.semaphore_wait(barrier, group + 1)
 
     def send_row(c, carry):
@@ -530,6 +582,14 @@
         return carry
 
     lax.fori_loop(0, chunks, send_row, 0)
+    diff_load.wait()
+    turned = lax.dot_general(
+        diff_s[...], axial_ref[...], (((0,), (0,)), ((), ())), preferred_element_type=F32
+    ).astype(BF)
+    for s in range(group):
+        first = pl.multiple_of(near + s * own_axial, own_axial)
+        forward_s[s * half : s * half + own_axial] = axial_ref[pl.ds(first, own_axial), :]
+        forward_s[s * half + own_axial : (s + 1) * half] = turned[s * own_axial : (s + 1) * own_axial]
 
     def radial_part(c):
         own_load(c).wait()
@@ -542,8 +602,7 @@
 
         @pl.when(c >= 2)
         def _():
-            for k in others:
-                ahead_copy(c - 2, k).wait_send()
+            each_peer(lambda kind, k: ahead_copy(c - 2, kind, k).wait_send())
 
         row_copy(c).wait_recv()
         for m in range(count):
@@ -556,62 +615,88 @@
                 preferred_element_type=F32,
             )
             field_s[mode] = hat.astype(BF)
-        mine = pl.multiple_of(place * block, block)
-        lines_s[place, span(c)] = field_s[span(c), pl.ds(mine, block), :]
-        for k in others:
-            ahead_copy(c, k).start()
-
-    def axial_part(c):
-        for k in others:
-            ahead_copy(c, k).wait_recv()
+        each_peer(lambda kind, k: ahead_copy(c, kind, k).start())
+        for kind in range(2):
+
+            @pl.when(mine == kind)
+            def _():
+                part = field_s[span(c), rows_of(kind, seat), :]
+                lines_s[place, span(c), : sizes[kind], :] = part
+
+    def axial_part(own_kind, c):
+        size = sizes[own_kind]
+        rows = count * size
+        each_peer(lambda kind, k: ahead_come(c, own_kind, kind, k).wait_recv())
 
         @pl.when(c >= 2)
         def _():
-            cross_copy(c - 2).wait_send()
-
-        first = pl.multiple_of(c * rows, rows)
-        eigen = radial_ref[pl.ds(first, rows), :] + axial_ref[...] + HEAT_OFFSET
-        returned = []
-        for p in range(2):
-            lines = jnp.concatenate(
-                [
-                    lines_s[s, span(c), :, p * half : (p + 1) * half].reshape(rows, half)
-                    for s in range(group)
-                ],
-                axis=1,
+            cross_copy(c - 2, own_kind).wait_send()
+
+        lines = jnp.concatenate(
+            [
+                jnp.concatenate(
+                    [
+                        lines_s[s, span(c), :size, p * half : (p + 1) * half].reshape(rows, half)
+                        for s in range(group)
+                    ],
+                    axis=1,
+                )
+                for p in range(2)
+            ],
+            axis=0,
+        )
+        coefficients = jnp.dot(lines, forward_s[...], preferred_element_type=F32)
+        first = starts[own_kind] + seat * size
+        chosen = (
+            lax.broadcasted_iota(jnp.int32, (size, radial), 1)
+            == lax.broadcasted_iota(jnp.int32, (size, radial), 0) + first
+        )
+        eigen = jnp.concatenate(
+            [
+                jnp.sum(
+                    jnp.where(chosen, radial_ref[pl.ds(c * count + m, 1), :], 0.0),
+                    axis=1,
+                    keepdims=True,
+                )
+                for m in range(count)
+            ],
+            axis=0,
+        )
+        eigen = eigen + eig_ref[...] + HEAT_OFFSET
+        coefficients = jnp.concatenate(
+            [(coefficients[p * rows : (p + 1) * rows] / eigen).astype(BF) for p in range(2)], axis=0
+        )
+        for far in (True, False):
+            first = pl.multiple_of((1 - side if far else side) * points, points)
+            returned = lax.dot_general(
+                coefficients,
+                axial_ref[pl.ds(first, points), :],
+                (((1,), (1,)), ((), ())),
+                preferred_element_type=F32,
             )
-            coefficients = jnp.dot(lines, forward_ref[...], preferred_element_type=F32) / eigen
-            returned.append(
-                lax.dot_general(
-                    coefficients.astype(BF),
-                    back_ref[...],
-                    (((1,), (1,)), ((), ())),
-                    preferred_element_type=F32,
-                )
-            )
-        for s in range(2 * group):
-            own = slice(s * quarter, (s + 1) * quarter)
-            pair = jnp.concatenate([returned[0][:, own], returned[1][:, own]], axis=1)
-            pair = pair.reshape(count, block, half)
-            if s < group:
-                part_s[c % part_s.shape[0], s] = pair
-            else:
-                cross_o[c % 2, s - group] = pair.astype(BF)
-        cross_copy(c).start()
-
-    def add_part(c):
-        cross_copy(c).wait_recv()
+            for s in range(group):
+                own = slice(s * own_axial, (s + 1) * own_axial)
+                pair = jnp.concatenate([returned[:rows, own], returned[rows:, own]], axis=1)
+                pair = pair.reshape(count, size, half)
+                if far:
+                    cross_o[c % 2, s, :, :size] = pair.astype(BF)
+                else:
+                    part_s[c % part_s.shape[0], s, :, :size] = pair
+            if far:
+                cross_copy(c, own_kind).start()
+
+    def add_part(own_kind, c):
+        size = sizes[own_kind]
+        cross_copy(c, own_kind).wait_recv()
 
         @pl.when(c >= 2)
         def _():
-            for k in others:
-                back_copy(c - 2, k).wait_send()
-
-        total = part_s[c % part_s.shape[0]] + cross_s[c].astype(F32)
-        back_o[c % 2] = total.astype(BF)
-        back_s[place, span(c)] = back_o[c % 2, place]
-        for k in others:
-            back_copy(c, k).start()
+            each_peer(lambda kind, k: back_copy(c - 2, own_kind, kind, k).wait_send())
+
+        total = part_s[c % part_s.shape[0], :, :, :size] + cross_s[c, :, :, :size].astype(F32)
+        back_o[c % 2, :, :, :size] = total.astype(BF)
+        each_peer(lambda kind, k: back_copy(c, own_kind, kind, k).start())
+        back_s[span(c), rows_of(own_kind, seat), :] = back_o[c % 2, place, :, :size]
 
     def last_part(c):
         again_load(c).wait()
@@ -624,23 +709,28 @@
         def _():
             out_copy(c - 2).wait()
 
-        for k in others:
-            back_copy(c, k).wait_recv()
+        each_peer(lambda kind, k: back_come(c, kind, k).wait_recv())
         for m in range(count):
-            lines = back_s[:, c * count + m].reshape(group * block, half)
             out_s[c % 2, m] = lax.dot_general(
-                lines, again_s[c % 2, m], (((0,), (1,)), ((), ())), preferred_element_type=F32
+                back_s[c * count + m],
+                again_s[c % 2, m],
+                (((0,), (1,)), ((), ())),
+                preferred_element_type=F32,
             ).reshape(out_s.shape[2:])
         out_copy(c).start()
 
     def step(s, carry):
-        for part, lag in (
-            (radial_part, 0),
-            (add_part, lag_add),
-            (axial_part, lag_axial),
-            (last_part, lag_last),
-        ):
-            pl.when((s >= lag) & (s < chunks + lag))(functools.partial(part, s - lag))
+        def live(lag):
+            return (s >= lag) & (s < chunks + lag)
+
+        pl.when(live(0))(functools.partial(radial_part, s))
+        for kind in range(2):
+            add = functools.partial(add_part, kind, s - lag_add)
+            pl.when(live(lag_add) & (mine == kind))(add)
+        for kind in range(2):
+            solve_lines = functools.partial(axial_part, kind, s - lag_axial)
+            pl.when(live(lag_axial) & (mine == kind))(solve_lines)
+        pl.when(live(lag_last))(functools.partial(last_part, s - lag_last))
         return carry
 
     lax.fori_loop(0, chunks + lag_last, step, 0)
@@ -651,68 +741,74 @@
 
     lax.fori_loop(0, chunks, row_done, 0)
     for c in range(chunks - 2, chunks):
-        for k in others:
-            ahead_copy(c, k).wait_send()
-            back_copy(c, k).wait_send()
-        cross_copy(c).wait_send()
+        each_peer(lambda kind, k: ahead_copy(c, kind, k).wait_send())
+        for own_kind in range(2):
+
+            @pl.when(mine == own_kind)
+            def _():
+                each_peer(lambda kind, k: back_copy(c, own_kind, kind, k).wait_send())
+                cross_copy(c, own_kind).wait_send()
+
         out_copy(c).wait()
 
 
-def solve(own, other, basis, forward, back, radial_values, axial_eig, group, chunks, lags):
+def solve(own, other, basis, axial_diff, axial_basis, radial_eig, axial_eig, group, chunks, lags):
     modes, radial, _ = basis.shape
     width = own.shape[1]
-    points = forward.shape[1]
-    block = radial // group
+    points = axial_basis.shape[0]
+    team = group // 2
+    big = radial // group * BIG_SHARE // 4
     count = modes // chunks
     half = width // 2
+    own_axial = width // 4
     anywhere = pl.BlockSpec(memory_space=pl.ANY)
     vmem = pl.BlockSpec(memory_space=pltpu.VMEM)
-    own_axial = width // 4
     dma = pltpu.SemaphoreType.DMA
-    lines = 2 * modes * block
-    sent = 2 * modes * radial * width * 3
     return pl.pallas_call(
         functools.partial(solve_kernel, chunks, lags),
-        in_specs=[anywhere] * 3 + [vmem] * 4,
+        in_specs=[anywhere] * 4 + [vmem] * 3,
         out_specs=anywhere,
         out_shape=jax.ShapeDtypeStruct((modes, 2, own_axial, radial), F32),
         scratch_shapes=[
             pltpu.VMEM((modes, width, radial), BF),
-            pltpu.VMEM((group, modes, block, width), BF),
-            pltpu.VMEM((chunks, group, count, block, half), BF),
-            pltpu.VMEM((group, modes, block, half), BF),
-            pltpu.VMEM((lags[1] - lags[0], group, count, block, half), F32),
-            pltpu.VMEM((2, group, count, block, half), BF),
-            pltpu.VMEM((2, group, count, block, half), BF),
+            pltpu.VMEM((group, modes, big, width), BF),
+            pltpu.VMEM((chunks, group, count, big, half), BF),
+            pltpu.VMEM((modes, radial, half), BF),
+            pltpu.VMEM((lags[1] - lags[0], group, count, big, half), F32),
+            pltpu.VMEM((2, group, count, big, half), BF),
+            pltpu.VMEM((2, group, count, big, half), BF),
             pltpu.VMEM((2, count, width, radial), BF),
             pltpu.VMEM((2, count, radial, radial), BF),
             pltpu.VMEM((2, count, radial, radial), BF),
             pltpu.VMEM((2, count, 2, own_axial, radial), F32),
+            pltpu.VMEM((points, points), BF),
+            pltpu.VMEM((points, points // 2), BF),
             dma((chunks,)),
             dma((chunks,)),
-            dma((2, group)),
-            dma((chunks, group)),
+            dma((2, 2, team)),
+            dma((chunks, 2, team)),
             dma((2,)),
             dma((chunks,)),
-            dma((2, group)),
-            dma((chunks, group)),
-            dma((3, 2)),
+            dma((2, 2, team)),
+            dma((chunks, 2, team)),
+            dma((4, 2)),
             dma((2,)),
         ],
         compiler_params=pltpu.CompilerParams(
-            collective_id=0, has_side_effects=True, vmem_limit_bytes=63 * 2**20
+            collective_id=0, has_side_effects=True, vmem_limit_bytes=67043328
         ),
         cost_estimate=pl.CostEstimate(
-            flops=4 * lines * points * points + 6 * modes * radial * radial * width,
-            bytes_accessed=sent,
+            flops=8 * modes * radial // group * points * points,
+            bytes_accessed=6 * modes * radial * width,
             transcendentals=0,
         ),
         name="solve",
-    )(own, other, basis, forward, back, radial_values.reshape(modes * block, 1), axial_eig[None])
-
-
-CHUNK_MODES = 7
+    )(own, other, basis, axial_diff, axial_basis, radial_eig, axial_eig[None])
+
+
+CHUNK_MODES = 3
 LAGS = (1, 2, 3)
+BIG_SHARE = 6
 
 
 def fused_body(
@@ -729,39 +825,31 @@
     row_total = lax.axis_size("row")
     group = lax.axis_size("col") // 2
     row_place = lax.axis_index("row")
-    col_place = lax.axis_index("col")
-    side, place = col_place // group, col_place % group
     modes = radial_basis.shape[0]
     angles, own_axial, radial_points = adj_temp.shape
-    axial_points = axial_basis.shape[0]
     circle = angles * row_total
-    block = radial_points // group
-    dests = (row_place, 1 - row_place)
+    padded = round_up(modes, 8)
+    firsts = [row_place * modes, (1 - row_place) * modes]
     tables = jnp.stack(
-        [wave_rows(d * modes, modes, row_place * angles, angles, circle) for d in dests]
+        [wave_rows(first, padded, row_place * angles, angles, circle) for first in firsts]
     )
     mode_values = jnp.stack(
-        [(d * modes + jnp.arange(modes, dtype=jnp.int32)).astype(F32) for d in dests]
+        [(first + jnp.arange(padded, dtype=jnp.int32)).astype(F32) for first in firsts]
     )
     own, other = both_sums(
-        velocity, adj_temp, radial_div, tables, mode_values, reciprocal_distance
-    )
-    own = own.reshape(modes, 4 * own_axial, radial_points)
-    other = other.reshape(modes, 4 * own_axial, radial_points)
-
-    half_points = axial_points // 2
-    near = lax.dynamic_slice_in_dim(axial_basis, side * half_points, half_points, 0)
-    far = lax.dynamic_slice_in_dim(axial_basis, (1 - side) * half_points, half_points, 0)
-    near_diff = lax.dynamic_slice_in_dim(axial_diff, side * half_points, half_points, 1)
-    turned = jnp.einsum("zj,zk->jk", near_diff, axial_basis, preferred_element_type=F32).astype(BF)
-    forward = jnp.stack(
-        [x.reshape(group, own_axial, axial_points) for x in (near, turned)], axis=1
-    ).reshape(axial_points, axial_points)
-    back = jnp.concatenate([near, far], axis=0)
-    radial_values = lax.dynamic_slice_in_dim(radial_eig, place * block, block, 1)
-    chunks = modes // CHUNK_MODES
+        velocity, adj_temp, radial_div, tables, mode_values, reciprocal_distance, modes
+    )
     return solve(
-        own, other, radial_basis, forward, back, radial_values, axial_eig, group, chunks, LAGS
+        own.reshape(modes, 4 * own_axial, radial_points),
+        other.reshape(modes, 4 * own_axial, radial_points),
+        radial_basis,
+        axial_diff,
+        axial_basis,
+        radial_eig,
+        axial_eig,
+        group,
+        modes // CHUNK_MODES,
+        LAGS,
     )
 
 

time: 418 us -> 362 us (0.87)
  Pallas kernels: 394 us -> 349 us
  local copies, waits for them, and re-layouts: 15.2 us -> 10.2 us
    pallas_call x1, Pallas kernels: 347 us -> 303 us  [solve(): pl.pallas_call(functools.partial(solve_kernel, chunks, lags), in_specs=[a...]
    unnamed x7 -> x1, local copies, waits for them, and re-layouts: 11.1 us -> 10.2 us
where the time goes in v1:
time: 362 us
  Pallas kernels  349 us (96%)
  local copies, waits for them, and re-layouts  10.2 us (3%)
    pallas_call x1, Pallas kernels, solve(): pl.pallas_call(functools.partial(solve_kernel, chunks, lags), in_specs=[a...  303 us
    pallas_call x1, Pallas kernels, both_sums(): pl.pallas_call(functools.partial(both_sums_kernel, modes, padded), grid=(...  46.3 us
    unnamed x1, local copies, waits for them, and re-layouts  10.2 us

profile of v1, /device:TPU:0, one launch (start us, length us, event | category | flops | bytes accessed | tf_op | source)
XLA Modules:
  0.0 362.2 jit_solution(5525610810093359629)
XLA Ops:
  0.0 0.8 fusion.6
  0.9 0.7 maximum_maximum_fusion
  1.6 1.4 broadcast_multiply_fusion.scale_ref
  3.0 46.3 %sums.1 = (bf16[84,2,2,64,256]{4,3,2,1,0:T(8,128)(2,1)}, bf16[84,2,2,64,256]{4,3,2,1,0:T(8,128)(2,1)}) custom-call(bf16[3,256,64,256]{3,2,1,0:T(8,128)(2,1)} %vel_ref.1, bf16[256,64,256]{2,1,0:T(8,128)(2,1)} %adj_ref.1, bf16[256,256]{1,0:T(8,128)(2,1)} %div_ref.1, bf16[352,256]{1,0:T(8,128)(2,1)} %bitcast.14, f32[2,88,256]{2,1,0:T(8,128)} %broadcast_multiply_fusion.scale_ref), custom_call_target="tpu_custom_call" | custom-call | flops 11005853696 | bytes 33554432 | tf_op jit(solution)/shard_map/sums/pallas_call | solution.py:383
  49.3 302.7 %solve.1 = f32[84,2,64,256]{3,2,1,0:T(8,128)} custom-call(bf16[84,256,256]{2,1,0:T(8,128)(2,1)} %bitcast.16, bf16[84,256,256]{2,1,0:T(8,128)(2,1)} %bitcast.17, bf16[84,256,256]{2,1,0:T(8,128)(2,1)} %basis_hbm.1, bf16[1024,1024]{1,0:T(8,128)(2,1)} %diff_hbm.1, bf16[1024,1024]{1,0:T(8,128)(2,1)} %axial_ref.1, f32[84,256]{1,0:T(8,128)} %radial_ref.1, ...), custom_call_target="tpu_custom_call" | custom-call | flops 22548578304 | bytes 33030144 | tf_op jit(solution)/shard_map/solve/pallas_call | solution.py:767
  352.0 10.2 %copy.11 = f32[84,2,64,256]{3,2,1,0:T(8,128)} copy(f32[84,2,64,256]{3,2,1,0:T(8,128)} %solve.1) | data formatting | bytes 22020096
  (4 shorter events, 0.0 us)

commit v2 on v1

--- a/solution.py
+++ b/solution.py
@@ -337,9 +337,8 @@
 def both_sums_kernel(modes, padded, vel_ref, adj_ref, div_ref, table_ref, scale_ref, *refs):
     *out_refs, field_s, sum_s = refs
     angles, block, radial = adj_ref.shape
-    adj = adj_ref[...].astype(F32)
     for f in range(3):
-        flux = (vel_ref[f].astype(F32) * adj).astype(BF)
+        flux = vel_ref[f] * adj_ref[...]
         if f == 0:
             moved = lax.dot_general(
                 flux.reshape(angles * block, radial),
@@ -347,7 +346,7 @@
                 (((1,), (1,)), ((), ())),
                 preferred_element_type=F32,
             ).reshape(angles, block, radial)
-            flux = (HEAT_OFFSET * adj + moved).astype(BF)
+            flux = (HEAT_OFFSET * adj_ref[...].astype(F32) + moved).astype(BF)
         field_s[f] = jnp.swapaxes(flux, 0, 1)
 
     def one(z, carry):
@@ -358,17 +357,17 @@
             re = slice(2 * d * padded, (2 * d + 1) * padded)
             im = slice((2 * d + 1) * padded, (2 * d + 2) * padded)
             scale = scale_ref[d]
-            sum_s[4 * d, z] = heat[re] - scale * turn[im]
-            sum_s[4 * d + 1, z] = flux[re]
-            sum_s[4 * d + 2, z] = heat[im] + scale * turn[re]
-            sum_s[4 * d + 3, z] = flux[im]
+            sum_s[4 * d, z] = (heat[re] - scale * turn[im]).astype(BF)
+            sum_s[4 * d + 1, z] = (flux[re]).astype(BF)
+            sum_s[4 * d + 2, z] = (heat[im] + scale * turn[re]).astype(BF)
+            sum_s[4 * d + 3, z] = (flux[im]).astype(BF)
         return carry
 
     lax.fori_loop(0, block, one, 0)
     for d, out_ref in enumerate(out_refs):
         for k in range(4):
             turned = jnp.swapaxes(sum_s[4 * d + k], 0, 1)
-            out_ref[:, k // 2, k % 2] = turned[:modes].astype(BF)
+            out_ref[:, k // 2, k % 2] = turned[:modes]
 
 
 def both_sums(
@@ -394,7 +393,7 @@
         out_shape=[jax.ShapeDtypeStruct((modes, 2, 2, own_axial, radial), BF)] * dests,
         scratch_shapes=[
             pltpu.VMEM((3, block, angles, radial), BF),
-            pltpu.VMEM((4 * dests, block, padded, radial), F32),
+            pltpu.VMEM((4 * dests, block, padded, radial), BF),
         ],
         compiler_params=pltpu.CompilerParams(vmem_limit_bytes=60 * 2**20),
         cost_estimate=pl.CostEstimate(
@@ -472,8 +471,10 @@
     def place_of(kind, k):
         return ((kind + 1 + side) % 2) * team + peer_seat(k)
 
-    def each_peer(act):
-        for kind in range(2):
+    solvers = [kind for kind in range(2) if sizes[kind]]
+
+    def each_peer(act, kinds=(0, 1)):
+        for kind in kinds:
             for k in range(team):
                 if k == 0:
                     pl.when(mine != kind)(functools.partial(act, kind, k))
@@ -602,7 +603,7 @@
 
         @pl.when(c >= 2)
         def _():
-            each_peer(lambda kind, k: ahead_copy(c - 2, kind, k).wait_send())
+            each_peer(lambda kind, k: ahead_copy(c - 2, kind, k).wait_send(), solvers)
 
         row_copy(c).wait_recv()
         for m in range(count):
@@ -615,8 +616,8 @@
                 preferred_element_type=F32,
             )
             field_s[mode] = hat.astype(BF)
-        each_peer(lambda kind, k: ahead_copy(c, kind, k).start())
-        for kind in range(2):
+        each_peer(lambda kind, k: ahead_copy(c, kind, k).start(), solvers)
+        for kind in solvers:
 
             @pl.when(mine == kind)
             def _():
@@ -709,14 +710,14 @@
         def _():
             out_copy(c - 2).wait()
 
-        each_peer(lambda kind, k: back_come(c, kind, k).wait_recv())
+        each_peer(lambda kind, k: back_come(c, kind, k).wait_recv(), solvers)
         for m in range(count):
             out_s[c % 2, m] = lax.dot_general(
                 back_s[c * count + m],
                 again_s[c % 2, m],
                 (((0,), (1,)), ((), ())),
                 preferred_element_type=F32,
-            ).reshape(out_s.shape[2:])
+            ).astype(BF).reshape(out_s.shape[2:])
         out_copy(c).start()
 
     def step(s, carry):
@@ -724,10 +725,10 @@
             return (s >= lag) & (s < chunks + lag)
 
         pl.when(live(0))(functools.partial(radial_part, s))
-        for kind in range(2):
+        for kind in solvers:
             add = functools.partial(add_part, kind, s - lag_add)
             pl.when(live(lag_add) & (mine == kind))(add)
-        for kind in range(2):
+        for kind in solvers:
             solve_lines = functools.partial(axial_part, kind, s - lag_axial)
             pl.when(live(lag_axial) & (mine == kind))(solve_lines)
         pl.when(live(lag_last))(functools.partial(last_part, s - lag_last))
@@ -741,8 +742,8 @@
 
     lax.fori_loop(0, chunks, row_done, 0)
     for c in range(chunks - 2, chunks):
-        each_peer(lambda kind, k: ahead_copy(c, kind, k).wait_send())
-        for own_kind in range(2):
+        each_peer(lambda kind, k: ahead_copy(c, kind, k).wait_send(), solvers)
+        for own_kind in solvers:
 
             @pl.when(mine == own_kind)
             def _():
@@ -768,7 +769,7 @@
         functools.partial(solve_kernel, chunks, lags),
         in_specs=[anywhere] * 4 + [vmem] * 3,
         out_specs=anywhere,
-        out_shape=jax.ShapeDtypeStruct((modes, 2, own_axial, radial), F32),
+        out_shape=jax.ShapeDtypeStruct((modes, 2, own_axial, radial), BF),
         scratch_shapes=[
             pltpu.VMEM((modes, width, radial), BF),
             pltpu.VMEM((group, modes, big, width), BF),
@@ -780,7 +781,7 @@
             pltpu.VMEM((2, count, width, radial), BF),
             pltpu.VMEM((2, count, radial, radial), BF),
             pltpu.VMEM((2, count, radial, radial), BF),
-            pltpu.VMEM((2, count, 2, own_axial, radial), F32),
+            pltpu.VMEM((2, count, 2, own_axial, radial), BF),
             pltpu.VMEM((points, points), BF),
             pltpu.VMEM((points, points // 2), BF),
             dma((chunks,)),
@@ -806,8 +807,8 @@
     )(own, other, basis, axial_diff, axial_basis, radial_eig, axial_eig[None])
 
 
-CHUNK_MODES = 3
-LAGS = (1, 2, 3)
+CHUNK_MODES = 2
+LAGS = (1, 3, 4)
 BIG_SHARE = 6
 
 
@@ -850,7 +851,7 @@
         group,
         modes // CHUNK_MODES,
         LAGS,
-    )
+    ).astype(F32)
 
 
 def solution(mesh):

time: 362 us -> 353 us (0.975)
  local copies, waits for them, and re-layouts: 10.2 us -> 0 us
  other arithmetic: 2.99 us -> 11.4 us
  Pallas kernels: 349 us -> 341 us
    unnamed x1 -> x0, local copies, waits for them, and re-layouts: 10.2 us -> none
    convert_element_type x0 -> x1, other arithmetic: none -> 8.42 us  [fused_body(): return solve(own.reshape(modes, 4 * own_axial, radial_points), other.resh...]
    pallas_call x1, Pallas kernels: 46.3 us -> 42.3 us  [both_sums(): pl.pallas_call(functools.partial(both_sums_kernel, modes, padded), grid=(...]
where the time goes in v2:
time: 353 us
  Pallas kernels  341 us (97%)
  other arithmetic  11.4 us (3%)
    pallas_call x1, Pallas kernels, solve(): pl.pallas_call(functools.partial(solve_kernel, chunks, lags), in_specs=[a...  299 us
    pallas_call x1, Pallas kernels, both_sums(): pl.pallas_call(functools.partial(both_sums_kernel, modes, padded), grid=(...  42.3 us
    convert_element_type x1, other arithmetic, fused_body(): return solve(own.reshape(modes, 4 * own_axial, radial_points), other.resh...  8.42 us

profile of v2, /device:TPU:0, one launch (start us, length us, event | category | flops | bytes accessed | tf_op | source)
XLA Modules:
  0.0 352.9 jit_solution(4702832327907955011)
XLA Ops:
  0.0 0.8 fusion.6
  0.9 0.7 maximum_maximum_fusion
  1.6 1.4 broadcast_multiply_fusion.scale_ref
  3.0 42.3 %sums.1 = (bf16[84,2,2,64,256]{4,3,2,1,0:T(8,128)(2,1)}, bf16[84,2,2,64,256]{4,3,2,1,0:T(8,128)(2,1)}) custom-call(bf16[3,256,64,256]{3,2,1,0:T(8,128)(2,1)} %vel_ref.1, bf16[256,64,256]{2,1,0:T(8,128)(2,1)} %adj_ref.1, bf16[256,256]{1,0:T(8,128)(2,1)} %div_ref.1, bf16[352,256]{1,0:T(8,128)(2,1)} %bitcast.14, f32[2,88,256]{2,1,0:T(8,128)} %broadcast_multiply_fusion.scale_ref), custom_call_target="tpu_custom_call" | custom-call | flops 11005853696 | bytes 33554432 | tf_op jit(solution)/shard_map/sums/pallas_call | solution.py:382
  45.3 299.2 %solve.1 = bf16[84,2,64,256]{3,2,1,0:T(8,128)(2,1)} custom-call(bf16[84,256,256]{2,1,0:T(8,128)(2,1)} %bitcast.16, bf16[84,256,256]{2,1,0:T(8,128)(2,1)} %bitcast.17, bf16[84,256,256]{2,1,0:T(8,128)(2,1)} %basis_hbm.1, bf16[1024,1024]{1,0:T(8,128)(2,1)} %diff_hbm.1, bf16[1024,1024]{1,0:T(8,128)(2,1)} %axial_ref.1, f32[84,256]{1,0:T(8,128)} %radial_ref.1, ...), custom_call_target="tpu_custom_call" | custom-call | flops 22548578304 | bytes 33030144 | tf_op jit(solution)/shard_map/solve/pallas_call | solution.py:768
  344.5 8.4 %convert_element_type.95 = f32[84,2,64,256]{3,2,1,0:T(8,128)} convert(bf16[84,2,64,256]{3,2,1,0:T(8,128)(2,1)} %solve.1) | non-fusion elementwise | flops 2752512 | bytes 16515072 | tf_op jit(solution)/shard_map/convert_element_type | solution.py:854
  (4 shorter events, 0.0 us)
